TPU v7x, 512 devices: a whole 4x8x8 slice. The times are simulated.
512 devices in a mesh: ens: 16 (over x, y_lo), lat: 32 (over y_hi, z, core).
Axes of the slice: x: 4, y: 8 (y_hi: 2, y_lo: 4; y = y_hi * 4 + y_lo), z: 8, core: 2. Of those that a mesh axis runs over, the one named last changes fastest.
Arguments:
- features: bfloat16 [128, 128, 128], P('lat'), may hold values from -6 to 6
- random_perturbation: bfloat16 [16, 128, 128, 128], P('ens', 'lat'), may hold values from -6 to 6
- observed_truth: float32 [69, 128, 128], P(None, 'lat'), may hold values from -6 to 6
- stencil_taps: float32 [49, 128], replicated, may hold values from -0.875 to 0.875
- affine_factor: float32 [128], replicated, may hold values from 0.5 to 1.5
- widen_matrix: bfloat16 [512, 128], P('lat'), may hold values from -0.5 to 0.5
- shrink_matrix: bfloat16 [512, 128], P('lat'), may hold values from -0.25 to 0.25
- readout_matrix: bfloat16 [69, 128], replicated, may hold values from -0.5 to 0.5
Outputs:
- crps_score: float32 [], replicated
- stencil_taps_sensitivity: float32 [49, 128], replicated
- affine_factor_sensitivity: float32 [128], replicated
- widen_matrix_sensitivity: float32 [512, 128], P('lat')
- shrink_matrix_sensitivity: float32 [512, 128], P('lat')
- readout_matrix_sensitivity: float32 [69, 128], replicated
- sample_outlook: bfloat16 [16, 69, 128, 128], P('ens', None, 'lat')
- sample_average_spread: float32 [16, 69, 128, 128], P('ens', None, 'lat')
All inputs are finite; a program needn't handle non-finite values.
Results may differ from a plain program's by a relative error of at most 0.0024.
The roundings to bfloat16 on the way count: a program that leaves them out, or rounds other values in their place, can miss the bound.
Values may be sent and summed in bfloat16 or wider, within the bound.
No kernel may reach another device: no remote copies, remote signals or barrier semaphores. Data moves between devices by JAX's collectives and lax.ppermute only.
A program may use at most 64 MiB of HBM per device.

v0:
```python
import math
import jax
import jax.numpy as jnp
from jax import lax
from jax.sharding import PartitionSpec as P

STENCIL_SIDE = 7
SQRT_TWO_PI = 0.7978845608028654
CUBIC = 0.044715
EPSILON = 1e-06
SMOOTHING = 0.01


def extended(cells, sides, width):
    for axis, dim in sides:
        count = lax.axis_size(axis)
        ends = count - 1
        head = lax.slice_in_dim(cells, 0, width, axis=dim)
        tail = lax.slice_in_dim(cells, cells.shape[dim] - width, cells.shape[dim], axis=dim)
        cells = jnp.concatenate(
            [
                lax.ppermute(tail, axis, [(i, (i + 1) % count) for i in range(ends)]),
                cells,
                lax.ppermute(head, axis, [((i + 1) % count, i) for i in range(ends)]),
            ],
            axis=dim,
        )
    return cells


def smooth_magnitude(value):
    return jnp.sqrt(value * value + SMOOTHING)


def smooth_slope(value):
    return value * lax.rsqrt(value * value + SMOOTHING)


def gelu_tanh(northern_margin):
    return (
        0.5
        * northern_margin
        * (
            1.0
            + jnp.tanh(
                SQRT_TWO_PI
                * (northern_margin + CUBIC * northern_margin * northern_margin * northern_margin)
            )
        )
    )


def gelu_slope(northern_margin):
    inner = jnp.tanh(
        SQRT_TWO_PI
        * (northern_margin + CUBIC * northern_margin * northern_margin * northern_margin)
    )
    return 0.5 * (1.0 + inner) + 0.5 * northern_margin * (1.0 - inner * inner) * SQRT_TWO_PI * (
        1.0 + 3.0 * CUBIC * northern_margin * northern_margin
    )


def depthwise(margin_extended, stencil_taps, meridian_slab):
    half = STENCIL_SIDE // 2
    wide = margin_extended.astype(jnp.float32)
    axis_rows = wide.ndim - 3
    result = jnp.zeros(
        wide.shape[:axis_rows] + (meridian_slab,) + wide.shape[axis_rows + 1 :], jnp.float32
    )
    for offset_row in range(STENCIL_SIDE):
        band = lax.slice_in_dim(wide, offset_row, offset_row + meridian_slab, axis=axis_rows)
        for offset_col in range(STENCIL_SIDE):
            result = result + stencil_taps[offset_row * STENCIL_SIDE + offset_col] * jnp.roll(
                band, half - offset_col, axis=-2
            )
    return result


def kernel_grad(margin_extended, upstream, meridian_slab):
    half = STENCIL_SIDE // 2
    wide = margin_extended.astype(jnp.float32)
    axis_rows = wide.ndim - 3
    channels = upstream.shape[-1]
    taps = []
    for offset_row in range(STENCIL_SIDE):
        band = lax.slice_in_dim(wide, offset_row, offset_row + meridian_slab, axis=axis_rows)
        for offset_col in range(STENCIL_SIDE):
            shifted = jnp.roll(band, half - offset_col, axis=-2)
            taps.append(jnp.sum((upstream * shifted).reshape(-1, channels), axis=0))
    return jnp.stack(taps)


def normalize(depth_out):
    centre = jnp.mean(depth_out, axis=-1, keepdims=True)
    centred = depth_out - centre
    variance = jnp.mean(centred * centred, axis=-1, keepdims=True)
    reciprocal_spread = lax.rsqrt(variance + EPSILON)
    return (centred * reciprocal_spread, reciprocal_spread)


def pair_terms(carry, owned_subset, piece):

    def one_pair(totals, other):
        gap = owned_subset - other.astype(jnp.float32)[None]
        return ((totals[0] + smooth_magnitude(gap), totals[1] + smooth_slope(gap)), None)

    carry, ignored_entry = lax.scan(one_pair, carry, piece)
    return carry


def on_device(
    features,
    random_perturbation,
    observed_truth,
    stencil_taps,
    affine_factor,
    widen_matrix,
    shrink_matrix,
    readout_matrix,
):
    sample_count, meridian_slab, zonal_points, channels = random_perturbation.shape
    outlook_quantities = readout_matrix.shape[0]
    half = STENCIL_SIDE // 2
    latitudes = meridian_slab * lax.axis_size("lat")
    ensemble = sample_count * lax.axis_size("ens")
    point_tally = meridian_slab * zonal_points
    planar_map = (
        features[None].astype(jnp.float32) + random_perturbation.astype(jnp.float32)
    ).astype(jnp.bfloat16)
    margin_extended = extended(planar_map, (("lat", 1),), half)
    up_full, down_full = (
        lax.all_gather(widen_matrix, "lat", axis=0, tiled=True),
        lax.all_gather(shrink_matrix, "lat", axis=0, tiled=True),
    )
    depth_out = depthwise(margin_extended, stencil_taps, meridian_slab)
    factor_multiplied, reciprocal_spread = normalize(depth_out)
    standardized_activation = (
        (affine_factor * factor_multiplied)
        .astype(jnp.bfloat16)
        .reshape(sample_count * point_tally, channels)
    )
    northern_margin = lax.dot_general(
        standardized_activation,
        up_full,
        (((1,), (1,)), ((), ())),
        preferred_element_type=jnp.float32,
    )
    nonlinear_response = gelu_tanh(northern_margin).astype(jnp.bfloat16)
    mixed = jnp.dot(nonlinear_response, down_full, preferred_element_type=jnp.float32)
    skip_activation = (
        planar_map.reshape(sample_count * point_tally, channels).astype(jnp.float32) + mixed
    ).astype(jnp.bfloat16)
    residual_row_block = skip_activation.reshape(sample_count, point_tally, channels)
    sample_outlook = jnp.einsum(
        "au,blu->bal", readout_matrix, residual_row_block, preferred_element_type=jnp.float32
    )
    sample_outlook = sample_outlook.astype(jnp.bfloat16).reshape(
        sample_count, outlook_quantities, meridian_slab, zonal_points
    )
    row_index = (
        lax.axis_index("lat") * meridian_slab + jnp.arange(meridian_slab, dtype=jnp.int32)
    ).astype(jnp.float32)
    area = jnp.cos(math.pi * ((row_index + 0.5) / latitudes - 0.5))
    weight = (area * (1.0 / (latitudes * zonal_points)))[None, None, :, None]
    pair_norm = 1.0 / (ensemble * (ensemble - 1))
    owned_subset = sample_outlook.astype(jnp.float32)
    blank_buffer = jnp.zeros_like(owned_subset)
    spread, ranks = pair_terms(
        (blank_buffer, blank_buffer),
        owned_subset,
        lax.all_gather(sample_outlook, "ens", axis=0, tiled=True),
    )
    miss = owned_subset - observed_truth[None]
    loss_part = jnp.sum(weight * (smooth_magnitude(miss) / ensemble - 0.5 * pair_norm * spread))
    carried_signal = (weight * (smooth_slope(miss) / ensemble - pair_norm * ranks)).astype(
        jnp.bfloat16
    )
    carried_signal = carried_signal.reshape(sample_count, outlook_quantities, point_tally)
    sample_average_spread = spread / (ensemble - 1)
    readout_matrix_sensitivity = jnp.einsum(
        "mvp,mpc->vc", carried_signal, residual_row_block, preferred_element_type=jnp.float32
    )
    back_residual = jnp.einsum(
        "mvp,vc->mpc", carried_signal, readout_matrix, preferred_element_type=jnp.float32
    )
    back_residual = back_residual.astype(jnp.bfloat16).reshape(sample_count * point_tally, channels)
    shrink_matrix_sensitivity = lax.dot_general(
        nonlinear_response,
        back_residual,
        (((0,), (0,)), ((), ())),
        preferred_element_type=jnp.float32,
    )
    back_gate = lax.dot_general(
        back_residual, down_full, (((1,), (1,)), ((), ())), preferred_element_type=jnp.float32
    )
    back_upper = (back_gate * gelu_slope(northern_margin)).astype(jnp.bfloat16)
    widen_matrix_sensitivity = lax.dot_general(
        back_upper,
        standardized_activation,
        (((0,), (0,)), ((), ())),
        preferred_element_type=jnp.float32,
    )
    back_norm = jnp.dot(back_upper, up_full, preferred_element_type=jnp.float32).reshape(
        sample_count, meridian_slab, zonal_points, channels
    )
    affine_factor_sensitivity = jnp.sum(
        (back_norm * factor_multiplied).reshape(-1, channels), axis=0
    )
    back_scaled = back_norm * affine_factor
    back_depth = reciprocal_spread * (
        back_scaled
        - jnp.mean(back_scaled, axis=-1, keepdims=True)
        - factor_multiplied * jnp.mean(back_scaled * factor_multiplied, axis=-1, keepdims=True)
    )
    stencil_taps_sensitivity = kernel_grad(margin_extended, back_depth, meridian_slab)
    summed_up, summed_down = lax.psum((widen_matrix_sensitivity, shrink_matrix_sensitivity), "ens")
    owned_up, owned_down = (
        lax.psum_scatter(summed_up, "lat", scatter_dimension=0, tiled=True),
        lax.psum_scatter(summed_down, "lat", scatter_dimension=0, tiled=True),
    )
    crps_score, total_out, total_gain, total_kernel = lax.psum(
        (
            loss_part,
            readout_matrix_sensitivity,
            affine_factor_sensitivity,
            stencil_taps_sensitivity,
        ),
        ("ens", "lat"),
    )
    return (
        crps_score,
        total_kernel,
        total_gain,
        owned_up,
        owned_down,
        total_out,
        sample_outlook,
        sample_average_spread,
    )


def solution(mesh):
    in_specs = (
        P("lat", None, None),
        P("ens", "lat", None, None),
        P(None, "lat", None),
        P(),
        P(),
        P("lat", None),
        P("lat", None),
        P(),
    )
    out_specs = (
        P(),
        P(),
        P(),
        P("lat", None),
        P("lat", None),
        P(),
        P("ens", None, "lat", None),
        P("ens", None, "lat", None),
    )
    return jax.shard_map(
        on_device, mesh=mesh, in_specs=in_specs, out_specs=out_specs, check_vma=False
    )
```

profile of v0, /device:TPU:64, one launch (start us, length us, event | category | flops | bytes accessed | tf_op | source)
XLA Modules:
  0.0 579.8 jit_solution(15327835750314781220)
XLA Ops:
  8.3 1.9 collective-permute-start
  10.2 3.6 collective-permute-start.1
  16.8 53.0 %all_gather.9 = bf16[512,128]{1,0:T(8,128)(2,1)S(1)} all-gather(bf16[16,128]{1,0:T(8,128)(2,1)} %param.15), channel_id=1, replica_groups=mesh['ens'=16,'lat'=32] {'lat'}, dimensions={0}, use_global_device_ids=true | all-gather | bytes 135168 | tf_op jit(solution)/shard_map/all_gather | solution.py:132
  69.8 54.0 %all_gather.10 = bf16[512,128]{1,0:T(8,128)(2,1)S(1)} all-gather(bf16[16,128]{1,0:T(8,128)(2,1)} %param.16), channel_id=1, replica_groups=mesh['ens'=16,'lat'=32] {'lat'}, dimensions={0}, use_global_device_ids=true | all-gather | bytes 135168 | tf_op jit(solution)/shard_map/all_gather | solution.py:133
  125.3 1.1 maximum_convert_fusion.37
  126.4 1.3 maximum_convert_fusion.34
  131.7 3.9 fusion.14
  136.1 1.4 multiply_convert_fusion
  141.5 74.7 %all-gather.2.cloned.1.call-done = bf16[16,69,4,128]{3,2,1,0:T(4,128)(2,1)} async-done(((bf16[1,69,4,128]{3,2,1,0:T(4,128)(2,1)}), bf16[16,69,4,128]{3,2,1,0:T(4,128)(2,1)}) %all-gather.2.cloned.1.call-update) | async-done | bytes 1130512 | tf_op jit(solution)/shard_map/all_gather | solution.py:171
  216.3 17.6 %while.13 = (s32[]{:T(128)}, f32[1,69,4,128]{3,2,1,0:T(4,128)S(1)}, f32[1,69,4,128]{3,2,1,0:T(4,128)S(1)}, bf16[16,69,4,128]{3,2,1,0:T(4,128)(2,1)}, f32[1,69,4,128]{3,2,1,0:T(4,128)S(1)}, /*index=5*/s32[]{:T(128)}, s32[]{:T(128)}) while((s32[]{:T(128)}, f32[1,69,4,128]{3,2,1,0:T(4,128)S(1)}, f32[1,69,4,128]{3,2,1,0:T(4,128)S(1)}, ...), condition=%wide.region_3.4_spmd.clone, body=%wide.region_2.3_spmd.clone.sunk | while | flops 317955 | bytes 777307 | solution.py:107
  216.3 1.1 select_add_fusion.3
  217.4 1.1 select_add_fusion.3
  218.5 1.1 select_add_fusion.3
  219.6 1.1 select_add_fusion.3
  220.7 1.1 select_add_fusion.3
  221.8 1.1 select_add_fusion.3
  222.9 1.1 select_add_fusion.3
  224.0 1.1 select_add_fusion.3
  225.1 1.1 select_add_fusion.3
  226.2 1.1 select_add_fusion.3
  227.3 1.1 select_add_fusion.3
  228.4 1.1 select_add_fusion.3
  232.8 1.1 select_add_fusion.3
  233.9 2.5 fusion.13
  237.8 2.1 fusion
  241.5 2.0 multiply_reduce_fusion.7
  243.5 1.8 multiply_reduce_fusion.17
  246.6 1.8 multiply_reduce_fusion.28
  251.4 99.0 %all-reduce = (f32[]{:T(128)}, f32[49,128]{1,0:T(8,128)}, f32[128]{0:T(128)}, f32[69,128]{1,0:T(8,128)}) all-reduce(f32[]{:T(128)} %get-tuple-element.219, f32[49,128]{1,0:T(8,128)S(1)} %stack.199, f32[128]{0:T(128)S(1)} %copy-done.86, f32[69,128]{1,0:T(8,128)S(1)} %fusion.22), channel_id=1, replica_groups=mesh['ens'=16,'lat'=32] {'ens','lat'}, use_global_device_ids=true, to_apply=%region_5.6 | all-reduce | flops 15233 | bytes 121864 | tf_op jit(solution)/shard_map/psum | solution.py:221
  350.3 20.7 %reduce-scatter.5.cloned.1.call-done = f32[16,128]{1,0:T(8,128)} async-done(((f32[512,128]{1,0:T(8,128)}), f32[16,128]{1,0:T(8,128)}) %reduce-scatter.5.cloned.1.call-update) | async-done | bytes 8208 | tf_op jit(solution)/shard_map/reduce_scatter | solution.py:219
  371.0 125.0 %reduce-scatter.3.cloned.1.call-done = f32[16,128]{1,0:T(8,128)} async-done(((f32[512,128]{1,0:T(8,128)}), f32[16,128]{1,0:T(8,128)}) %reduce-scatter.3.cloned.1.call-update) | async-done | bytes 8208 | tf_op jit(solution)/shard_map/reduce_scatter | solution.py:218
  496.0 77.3 %all-reduce.1 = (f32[16,128]{1,0:T(8,128)}, f32[16,128]{1,0:T(8,128)}) all-reduce(f32[16,128]{1,0:T(8,128)} %reduce-scatter.3.cloned.1.call-done, f32[16,128]{1,0:T(8,128)} %reduce-scatter.5.cloned.1.call-done), channel_id=1, replica_groups=mesh['ens'=16,'lat'=32] {'ens'}, use_global_device_ids=true, to_apply=%region_60.61 | all-reduce | flops 4096 | bytes 32768 | tf_op jit(solution)/shard_map/psum | solution.py:216
  (265 shorter events, 23.1 us)
Async XLA Ops:
  7.2 131.2 %copy-start = (bf16[69,128]{1,0:T(8,128)(2,1)S(1)}, bf16[69,128]{1,0:T(8,128)(2,1)}, u32[]{:S(2)}) copy-start(bf16[69,128]{1,0:T(8,128)(2,1)} %param.17) | copy-start | bytes 52996
  7.2 209.1 %all-gather.2.cloned.1.call-start = ((), (), s32[]{:S(2)}) async-start(), calls=%async_computation.2 | async-start | bytes 1201152 | tf_op jit(solution)/shard_map/all_gather | solution.py:171
  8.3 115.6 %collective-permute-start = (bf16[1,3,128,128]{3,2,1,0:T(8,128)(2,1)S(1)}, bf16[1,3,128,128]{3,2,1,0:T(8,128)(2,1)S(1)}, u32[]{:S(2)}, u32[]{:S(2)}) collective-permute-start(bf16[1,3,128,128]{3,2,1,0:T(8,128)(2,1)S(1)} %get-tuple-element.221), channel_id=1, source_target_pairs={{0,1},{1,2},{2,3},{3,4},{4,5},{5,6},{6,7},{7,8},{8,9},{9,10},{10,1... | collective-permute-start | bytes 294920 | tf_op jit(solution)/shard_map/ppermute | solution.py:22
  10.2 113.7 %collective-permute-start.1 = (bf16[1,3,128,128]{3,2,1,0:T(8,128)(2,1)S(1)}, bf16[1,3,128,128]{3,2,1,0:T(8,128)(2,1)S(1)}, u32[]{:S(2)}, u32[]{:S(2)}) collective-permute-start(bf16[1,3,128,128]{3,2,1,0:T(8,128)(2,1)S(1)} %get-tuple-element.222), channel_id=1, source_target_pairs={{1,0},{2,1},{3,2},{4,3},{5,4},{6,5},{7,6},{8,7},{9,8},{10,9},{11,1... | collective-permute-start | bytes 294920 | tf_op jit(solution)/shard_map/ppermute | solution.py:24
  69.8 66.3 %copy-start.68 = (bf16[512,128]{1,0:T(8,128)(2,1)}, bf16[512,128]{1,0:T(8,128)(2,1)S(1)}, u32[]{:S(2)}) copy-start(bf16[512,128]{1,0:T(8,128)(2,1)S(1)} %all_gather.9) | copy-start | bytes 393220
  123.8 13.7 %copy-start.70 = (bf16[512,128]{1,0:T(8,128)(2,1)}, bf16[512,128]{1,0:T(8,128)(2,1)S(1)}, u32[]{:S(2)}) copy-start(bf16[512,128]{1,0:T(8,128)(2,1)S(1)} %all_gather.10) | copy-start | bytes 393220
  124.2 7.1 %copy-start.7 = (f32[1,4,125,128]{3,2,1,0:T(8,128)}, f32[1,4,125,128]{3,2,1,0:T(8,128)S(1)}, u32[]{:S(2)}) copy-start(f32[1,4,125,128]{3,2,1,0:T(8,128)S(1)} %get-tuple-element.141) | copy-start | bytes 768004
  124.2 7.1 %copy-start.9 = (f32[1,4,125,128]{3,2,1,0:T(8,128)}, f32[1,4,125,128]{3,2,1,0:T(8,128)S(1)}, u32[]{:S(2)}) copy-start(f32[1,4,125,128]{3,2,1,0:T(8,128)S(1)} %get-tuple-element.142) | copy-start | bytes 768004
  124.2 7.1 %copy-start.11 = (f32[1,4,125,128]{3,2,1,0:T(8,128)}, f32[1,4,125,128]{3,2,1,0:T(8,128)S(1)}, u32[]{:S(2)}) copy-start(f32[1,4,125,128]{3,2,1,0:T(8,128)S(1)} %get-tuple-element.145) | copy-start | bytes 768004
  124.3 7.1 %copy-start.12 = (f32[1,4,125,128]{3,2,1,0:T(8,128)}, f32[1,4,125,128]{3,2,1,0:T(8,128)S(1)}, u32[]{:S(2)}) copy-start(f32[1,4,125,128]{3,2,1,0:T(8,128)S(1)} %get-tuple-element.146) | copy-start | bytes 768004
  124.3 7.1 %copy-start.18 = (f32[1,4,125,128]{3,2,1,0:T(8,128)}, f32[1,4,125,128]{3,2,1,0:T(8,128)S(1)}, u32[]{:S(2)}) copy-start(f32[1,4,125,128]{3,2,1,0:T(8,128)S(1)} %get-tuple-element.152) | copy-start | bytes 768004
  124.3 7.1 %copy-start.28 = (f32[1,4,125,128]{3,2,1,0:T(8,128)}, f32[1,4,125,128]{3,2,1,0:T(8,128)S(1)}, u32[]{:S(2)}) copy-start(f32[1,4,125,128]{3,2,1,0:T(8,128)S(1)} %get-tuple-element.147) | copy-start | bytes 768004
  124.3 7.1 %copy-start.44 = (f32[1,4,125,128]{3,2,1,0:T(8,128)}, f32[1,4,125,128]{3,2,1,0:T(8,128)S(1)}, u32[]{:S(2)}) copy-start(f32[1,4,125,128]{3,2,1,0:T(8,128)S(1)} %get-tuple-element.140) | copy-start | bytes 768004
  124.3 7.1 %copy-start.46 = (f32[1,4,125,128]{3,2,1,0:T(8,128)}, f32[1,4,125,128]{3,2,1,0:T(8,128)S(1)}, u32[]{:S(2)}) copy-start(f32[1,4,125,128]{3,2,1,0:T(8,128)S(1)} %get-tuple-element.143) | copy-start | bytes 768004
  124.3 7.1 %copy-start.48 = (f32[1,4,125,128]{3,2,1,0:T(8,128)}, f32[1,4,125,128]{3,2,1,0:T(8,128)S(1)}, u32[]{:S(2)}) copy-start(f32[1,4,125,128]{3,2,1,0:T(8,128)S(1)} %get-tuple-element.148) | copy-start | bytes 768004
  124.3 7.1 %copy-start.50 = (f32[1,4,125,128]{3,2,1,0:T(8,128)}, f32[1,4,125,128]{3,2,1,0:T(8,128)S(1)}, u32[]{:S(2)}) copy-start(f32[1,4,125,128]{3,2,1,0:T(8,128)S(1)} %get-tuple-element.151) | copy-start | bytes 768004
  124.6 6.8 %copy-start.13 = (f32[1,4,126,128]{3,2,1,0:T(8,128)}, f32[1,4,126,128]{3,2,1,0:T(8,128)S(1)}, u32[]{:S(2)}) copy-start(f32[1,4,126,128]{3,2,1,0:T(8,128)S(1)} %get-tuple-element.159) | copy-start | bytes 774148
  124.6 6.8 %copy-start.14 = (f32[1,4,126,128]{3,2,1,0:T(8,128)}, f32[1,4,126,128]{3,2,1,0:T(8,128)S(1)}, u32[]{:S(2)}) copy-start(f32[1,4,126,128]{3,2,1,0:T(8,128)S(1)} %get-tuple-element.161) | copy-start | bytes 774148
  124.7 6.8 %copy-start.15 = (f32[1,4,126,128]{3,2,1,0:T(8,128)}, f32[1,4,126,128]{3,2,1,0:T(8,128)S(1)}, u32[]{:S(2)}) copy-start(f32[1,4,126,128]{3,2,1,0:T(8,128)S(1)} %get-tuple-element.162) | copy-start | bytes 774148
  124.7 6.8 %copy-start.20 = (f32[1,4,126,128]{3,2,1,0:T(8,128)}, f32[1,4,126,128]{3,2,1,0:T(8,128)S(1)}, u32[]{:S(2)}) copy-start(f32[1,4,126,128]{3,2,1,0:T(8,128)S(1)} %get-tuple-element.160) | copy-start | bytes 774148
  124.7 6.8 %copy-start.22 = (f32[1,4,126,128]{3,2,1,0:T(8,128)}, f32[1,4,126,128]{3,2,1,0:T(8,128)S(1)}, u32[]{:S(2)}) copy-start(f32[1,4,126,128]{3,2,1,0:T(8,128)S(1)} %get-tuple-element.164) | copy-start | bytes 774148
  124.7 6.8 %copy-start.30 = (f32[1,4,126,128]{3,2,1,0:T(8,128)}, f32[1,4,126,128]{3,2,1,0:T(8,128)S(1)}, u32[]{:S(2)}) copy-start(f32[1,4,126,128]{3,2,1,0:T(8,128)S(1)} %get-tuple-element.154) | copy-start | bytes 774148
  124.7 6.8 %copy-start.32 = (f32[1,4,126,128]{3,2,1,0:T(8,128)}, f32[1,4,126,128]{3,2,1,0:T(8,128)S(1)}, u32[]{:S(2)}) copy-start(f32[1,4,126,128]{3,2,1,0:T(8,128)S(1)} %get-tuple-element.157) | copy-start | bytes 774148
  124.7 6.8 %copy-start.34 = (f32[1,4,126,128]{3,2,1,0:T(8,128)}, f32[1,4,126,128]{3,2,1,0:T(8,128)S(1)}, u32[]{:S(2)}) copy-start(f32[1,4,126,128]{3,2,1,0:T(8,128)S(1)} %get-tuple-element.166) | copy-start | bytes 774148
  125.2 10.4 %copy-start.58 = (f32[1,4,127,128]{3,2,1,0:T(8,128)}, f32[1,4,127,128]{3,2,1,0:T(8,128)S(1)}, u32[]{:S(2)}) copy-start(f32[1,4,127,128]{3,2,1,0:T(8,128)S(1)} %get-tuple-element.172) | copy-start | bytes 780292
  125.2 10.4 %copy-start.60 = (f32[1,4,127,128]{3,2,1,0:T(8,128)}, f32[1,4,127,128]{3,2,1,0:T(8,128)S(1)}, u32[]{:S(2)}) copy-start(f32[1,4,127,128]{3,2,1,0:T(8,128)S(1)} %get-tuple-element.180) | copy-start | bytes 780292
  125.2 10.3 %copy-start.74 = (f32[1,4,3,128]{3,2,1,0:T(4,128)}, f32[1,4,3,128]{3,2,1,0:T(4,128)S(1)}, u32[]{:S(2)}) copy-start(f32[1,4,3,128]{3,2,1,0:T(4,128)S(1)} %get-tuple-element.134) | copy-start | bytes 18436
  125.3 10.3 %copy-start.76 = (f32[1,4,3,128]{3,2,1,0:T(4,128)}, f32[1,4,3,128]{3,2,1,0:T(4,128)S(1)}, u32[]{:S(2)}) copy-start(f32[1,4,3,128]{3,2,1,0:T(4,128)S(1)} %get-tuple-element.135) | copy-start | bytes 18436
  125.3 10.3 %copy-start.78 = (f32[1,4,3,128]{3,2,1,0:T(4,128)}, f32[1,4,3,128]{3,2,1,0:T(4,128)S(1)}, u32[]{:S(2)}) copy-start(f32[1,4,3,128]{3,2,1,0:T(4,128)S(1)} %get-tuple-element.136) | copy-start | bytes 18436
  139.3 231.7 %reduce-scatter.5.cloned.1.call-start = ((), (), s32[]{:S(2)}) async-start(), calls=%async_computation.4 | async-start | bytes 270336 | tf_op jit(solution)/shard_map/reduce_scatter | solution.py:219
  216.3 17.6 %copy-start.105 = (f32[4]{0:T(128)S(1)}, f32[4]{0:T(128)}, u32[]{:S(2)}) copy-start(f32[4]{0:T(128)} %cosine_multiply_fusion) | copy-start | bytes 52
  246.5 249.5 %reduce-scatter.3.cloned.1.call-start = ((), (), s32[]{:S(2)}) async-start(), calls=%async_computation.3 | async-start | bytes 270336 | tf_op jit(solution)/shard_map/reduce_scatter | solution.py:218
  (79 other events, 203.0 us)
Sparse Core Ops, SparseCore 0:
  139.4 76.8 all-gather.1
  246.6 124.4 reduce-scatter.4
  375.6 120.3 reduce-scatter.2
where the time goes:
time: 581 us; the launch traced here: 580 us
  blocking collectives  283 us (49%)
  waiting for transfers between devices  220 us (38%)
  other arithmetic  41.3 us (7%)
  between operations  15.3 us (3%)
  matrix products  6.82 us (1%)
  local copies, waits for them, and re-layouts  6.71 us (1%)
    reduce_scatter x1, waiting for transfers between devices, on_device(): lax.psum_scatter(summed_up, 'lat', scatter_dimension=0, tiled=True)  125 us
    psum x1, blocking collectives, on_device(): lax.psum((loss_part, readout_matrix_sensitivity, affine_factor_sensitivit...  99 us
    psum x1, blocking collectives, on_device(): lax.psum((widen_matrix_sensitivity, shrink_matrix_sensitivity), 'ens')  77.3 us
    all_gather x1, waiting for transfers between devices, on_device(): lax.all_gather(sample_outlook, 'ens', axis=0, tiled=True)  74.7 us
    all_gather x1, blocking collectives, on_device(): lax.all_gather(shrink_matrix, 'lat', axis=0, tiled=True)  54 us
    all_gather x1, blocking collectives, on_device(): lax.all_gather(widen_matrix, 'lat', axis=0, tiled=True)  53 us
    reduce_scatter x1, waiting for transfers between devices, on_device(): lax.psum_scatter(summed_down, 'lat', scatter_dimension=0, tiled=True)  20.7 us
    add x16, other arithmetic, one_pair(): totals[1] + smooth_slope(gap)  17.3 us
  transfers between devices with their start and end apart: 5, of which 3 were waited for; matrix products, arithmetic and copies ran while one was open for 2% of the time, Pallas kernels for 0%

commit v1 on v0

--- a/solution.py
+++ b/solution.py
@@ -9,6 +9,11 @@
 CUBIC = 0.044715
 EPSILON = 1e-06
 SMOOTHING = 0.01
+
+
+def gather_over(value, axis, d):
+    stack = jnp.stack([value] * lax.axis_size(axis))
+    return jnp.concatenate(lax.all_to_all(stack, axis, 0, 0), axis=d)
 
 
 def extended(cells, sides, width):
@@ -166,9 +171,7 @@
     owned_subset = sample_outlook.astype(jnp.float32)
     blank_buffer = jnp.zeros_like(owned_subset)
     spread, ranks = pair_terms(
-        (blank_buffer, blank_buffer),
-        owned_subset,
-        lax.all_gather(sample_outlook, "ens", axis=0, tiled=True),
+        (blank_buffer, blank_buffer), owned_subset, gather_over(sample_outlook, "ens", 0)
     )
     miss = owned_subset - observed_truth[None]
     loss_part = jnp.sum(weight * (smooth_magnitude(miss) / ensemble - 0.5 * pair_norm * spread))

time: 581 us -> 532 us (0.916)
  waiting for transfers between devices: 220 us -> 172 us
  blocking collectives: 283 us -> 277 us
    all_gather x1 -> x0, waiting for transfers between devices: 74.7 us -> none  [on_device(): lax.all_gather(sample_outlook, 'ens', axis=0, tiled=True)]
    all_to_all x0 -> x1, waiting for transfers between devices: none -> 27.9 us  [gather_over(): return jnp.concatenate(lax.all_to_all(stack, axis, 0, 0), axis=d)]
where the time goes in v1:
time: 532 us; the launch traced here: 531 us
  blocking collectives  277 us (52%)
  waiting for transfers between devices  172 us (32%)
  other arithmetic  41.1 us (8%)
  between operations  15.6 us (3%)
  starting transfers between devices  10.4 us (2%)
  local copies, waits for them, and re-layouts  7.39 us (1%)
  matrix products  6.79 us (1%)
    reduce_scatter x1, waiting for transfers between devices, on_device(): lax.psum_scatter(summed_up, 'lat', scatter_dimension=0, tiled=True)  125 us
    psum x1, blocking collectives, on_device(): lax.psum((loss_part, readout_matrix_sensitivity, affine_factor_sensitivit...  93.3 us
    psum x1, blocking collectives, on_device(): lax.psum((widen_matrix_sensitivity, shrink_matrix_sensitivity), 'ens')  77.1 us
    all_gather x1, blocking collectives, on_device(): lax.all_gather(shrink_matrix, 'lat', axis=0, tiled=True)  54 us
    all_gather x1, blocking collectives, on_device(): lax.all_gather(widen_matrix, 'lat', axis=0, tiled=True)  53 us
    all_to_all x1, waiting for transfers between devices, gather_over(): return jnp.concatenate(lax.all_to_all(stack, axis, 0, 0), axis=d)  27.9 us
    reduce_scatter x1, waiting for transfers between devices, on_device(): lax.psum_scatter(summed_down, 'lat', scatter_dimension=0, tiled=True)  18.9 us
    add x16, other arithmetic, one_pair(): totals[1] + smooth_slope(gap)  17.3 us
  transfers between devices with their start and end apart: 5, of which 3 were waited for; matrix products, arithmetic and copies ran while one was open for 2% of the time, Pallas kernels for 0%

profile of v1, /device:TPU:64, one launch (start us, length us, event | category | flops | bytes accessed | tf_op | source)
XLA Modules:
  0.0 530.9 jit_solution(11647371463843942749)
XLA Ops:
  8.2 1.9 collective-permute-start
  10.2 3.6 collective-permute-start.1
  16.7 53.0 %all_gather.6 = bf16[512,128]{1,0:T(8,128)(2,1)S(1)} all-gather(bf16[16,128]{1,0:T(8,128)(2,1)} %param.15), channel_id=1, replica_groups=mesh['ens'=16,'lat'=32] {'lat'}, dimensions={0}, use_global_device_ids=true | all-gather | bytes 135168 | tf_op jit(solution)/shard_map/all_gather | solution.py:137
  69.8 54.0 %all_gather.7 = bf16[512,128]{1,0:T(8,128)(2,1)S(1)} all-gather(bf16[16,128]{1,0:T(8,128)(2,1)} %param.16), channel_id=1, replica_groups=mesh['ens'=16,'lat'=32] {'lat'}, dimensions={0}, use_global_device_ids=true | all-gather | bytes 135168 | tf_op jit(solution)/shard_map/all_gather | solution.py:138
  125.2 1.1 maximum_convert_fusion.37
  126.3 1.2 maximum_convert_fusion.34
  131.5 3.9 fusion.14
  135.9 1.4 multiply_convert_fusion
  138.4 1.3 stack.153
  139.7 4.8 all-to-all-start
  146.7 27.9 %all-to-all-done = bf16[16,1,69,4,128]{4,3,2,1,0:T(4,128)(2,1)} async-done(((bf16[16,1,69,4,128]{4,3,2,1,0:T(4,128)(2,1)}), bf16[16,1,69,4,128]{4,3,2,1,0:T(4,128)(2,1)}, u32[]{:S(2)}, u32[]{:S(2)}) %all-to-all-start) | async-done | bytes 1130528 | tf_op jit(solution)/shard_map/all_to_all | solution.py:16
  174.6 17.5 %while.13 = (s32[]{:T(128)}, f32[1,69,4,128]{3,2,1,0:T(4,128)S(1)}, f32[1,69,4,128]{3,2,1,0:T(4,128)S(1)}, bf16[16,69,4,128]{3,2,1,0:T(4,128)(2,1)}, f32[1,69,4,128]{3,2,1,0:T(4,128)S(1)}, /*index=5*/s32[]{:T(128)}, s32[]{:T(128)}) while((s32[]{:T(128)}, f32[1,69,4,128]{3,2,1,0:T(4,128)S(1)}, f32[1,69,4,128]{3,2,1,0:T(4,128)S(1)}, ...), condition=%wide.region_3.4_spmd.clone, body=%wide.region_2.3_spmd.clone.sunk | while | flops 317955 | bytes 777307 | solution.py:112
  175.7 1.1 select_add_fusion.3
  176.8 1.1 select_add_fusion.3
  177.9 1.1 select_add_fusion.3
  179.0 1.1 select_add_fusion.3
  180.1 1.1 select_add_fusion.3
  181.2 1.1 select_add_fusion.3
  182.3 1.1 select_add_fusion.3
  183.4 1.1 select_add_fusion.3
  184.5 1.1 select_add_fusion.3
  185.6 1.1 select_add_fusion.3
  190.0 1.1 select_add_fusion.3
  192.2 2.5 fusion.13
  196.1 2.1 fusion
  199.8 2.0 multiply_reduce_fusion.7
  201.9 1.7 multiply_reduce_fusion.17
  204.9 1.8 multiply_reduce_fusion.28
  209.7 93.3 %all-reduce = (f32[]{:T(128)}, f32[49,128]{1,0:T(8,128)}, f32[128]{0:T(128)}, f32[69,128]{1,0:T(8,128)}) all-reduce(f32[]{:T(128)} %get-tuple-element.219, f32[49,128]{1,0:T(8,128)S(1)} %stack.203, f32[128]{0:T(128)S(1)} %copy-done.86, f32[69,128]{1,0:T(8,128)S(1)} %fusion.22), channel_id=1, replica_groups=mesh['ens'=16,'lat'=32] {'ens','lat'}, use_global_device_ids=true, to_apply=%region_5.6 | all-reduce | flops 15233 | bytes 121864 | tf_op jit(solution)/shard_map/psum | solution.py:224
  303.0 18.9 %reduce-scatter.5.cloned.1.call-done = f32[16,128]{1,0:T(8,128)} async-done(((f32[512,128]{1,0:T(8,128)}), f32[16,128]{1,0:T(8,128)}) %reduce-scatter.5.cloned.1.call-update) | async-done | bytes 8208 | tf_op jit(solution)/shard_map/reduce_scatter | solution.py:222
  321.9 125.0 %reduce-scatter.3.cloned.1.call-done = f32[16,128]{1,0:T(8,128)} async-done(((f32[512,128]{1,0:T(8,128)}), f32[16,128]{1,0:T(8,128)}) %reduce-scatter.3.cloned.1.call-update) | async-done | bytes 8208 | tf_op jit(solution)/shard_map/reduce_scatter | solution.py:221
  446.9 77.1 %all-reduce.1 = (f32[16,128]{1,0:T(8,128)}, f32[16,128]{1,0:T(8,128)}) all-reduce(f32[16,128]{1,0:T(8,128)} %reduce-scatter.3.cloned.1.call-done, f32[16,128]{1,0:T(8,128)} %reduce-scatter.5.cloned.1.call-done), channel_id=1, replica_groups=mesh['ens'=16,'lat'=32] {'ens'}, use_global_device_ids=true, to_apply=%region_60.61 | all-reduce | flops 4096 | bytes 32768 | tf_op jit(solution)/shard_map/psum | solution.py:219
  (263 shorter events, 24.5 us)
Async XLA Ops:
  7.2 131.0 %copy-start = (bf16[69,128]{1,0:T(8,128)(2,1)S(1)}, bf16[69,128]{1,0:T(8,128)(2,1)}, u32[]{:S(2)}) copy-start(bf16[69,128]{1,0:T(8,128)(2,1)} %param.17) | copy-start | bytes 52996
  8.2 115.6 %collective-permute-start = (bf16[1,3,128,128]{3,2,1,0:T(8,128)(2,1)S(1)}, bf16[1,3,128,128]{3,2,1,0:T(8,128)(2,1)S(1)}, u32[]{:S(2)}, u32[]{:S(2)}) collective-permute-start(bf16[1,3,128,128]{3,2,1,0:T(8,128)(2,1)S(1)} %get-tuple-element.221), channel_id=1, source_target_pairs={{0,1},{1,2},{2,3},{3,4},{4,5},{5,6},{6,7},{7,8},{8,9},{9,10},{10,1... | collective-permute-start | bytes 294920 | tf_op jit(solution)/shard_map/ppermute | solution.py:27
  10.2 113.7 %collective-permute-start.1 = (bf16[1,3,128,128]{3,2,1,0:T(8,128)(2,1)S(1)}, bf16[1,3,128,128]{3,2,1,0:T(8,128)(2,1)S(1)}, u32[]{:S(2)}, u32[]{:S(2)}) collective-permute-start(bf16[1,3,128,128]{3,2,1,0:T(8,128)(2,1)S(1)} %get-tuple-element.222), channel_id=1, source_target_pairs={{1,0},{2,1},{3,2},{4,3},{5,4},{6,5},{7,6},{8,7},{9,8},{10,9},{11,1... | collective-permute-start | bytes 294920 | tf_op jit(solution)/shard_map/ppermute | solution.py:29
  69.8 66.2 %copy-start.68 = (bf16[512,128]{1,0:T(8,128)(2,1)}, bf16[512,128]{1,0:T(8,128)(2,1)S(1)}, u32[]{:S(2)}) copy-start(bf16[512,128]{1,0:T(8,128)(2,1)S(1)} %all_gather.6) | copy-start | bytes 393220
  123.8 13.5 %copy-start.70 = (bf16[512,128]{1,0:T(8,128)(2,1)}, bf16[512,128]{1,0:T(8,128)(2,1)S(1)}, u32[]{:S(2)}) copy-start(bf16[512,128]{1,0:T(8,128)(2,1)S(1)} %all_gather.7) | copy-start | bytes 393220
  124.2 7.0 %copy-start.7 = (f32[1,4,125,128]{3,2,1,0:T(8,128)}, f32[1,4,125,128]{3,2,1,0:T(8,128)S(1)}, u32[]{:S(2)}) copy-start(f32[1,4,125,128]{3,2,1,0:T(8,128)S(1)} %get-tuple-element.141) | copy-start | bytes 768004
  124.2 7.0 %copy-start.9 = (f32[1,4,125,128]{3,2,1,0:T(8,128)}, f32[1,4,125,128]{3,2,1,0:T(8,128)S(1)}, u32[]{:S(2)}) copy-start(f32[1,4,125,128]{3,2,1,0:T(8,128)S(1)} %get-tuple-element.142) | copy-start | bytes 768004
  124.2 6.9 %copy-start.11 = (f32[1,4,125,128]{3,2,1,0:T(8,128)}, f32[1,4,125,128]{3,2,1,0:T(8,128)S(1)}, u32[]{:S(2)}) copy-start(f32[1,4,125,128]{3,2,1,0:T(8,128)S(1)} %get-tuple-element.145) | copy-start | bytes 768004
  124.2 6.9 %copy-start.12 = (f32[1,4,125,128]{3,2,1,0:T(8,128)}, f32[1,4,125,128]{3,2,1,0:T(8,128)S(1)}, u32[]{:S(2)}) copy-start(f32[1,4,125,128]{3,2,1,0:T(8,128)S(1)} %get-tuple-element.146) | copy-start | bytes 768004
  124.2 6.9 %copy-start.18 = (f32[1,4,125,128]{3,2,1,0:T(8,128)}, f32[1,4,125,128]{3,2,1,0:T(8,128)S(1)}, u32[]{:S(2)}) copy-start(f32[1,4,125,128]{3,2,1,0:T(8,128)S(1)} %get-tuple-element.152) | copy-start | bytes 768004
  124.2 6.9 %copy-start.28 = (f32[1,4,125,128]{3,2,1,0:T(8,128)}, f32[1,4,125,128]{3,2,1,0:T(8,128)S(1)}, u32[]{:S(2)}) copy-start(f32[1,4,125,128]{3,2,1,0:T(8,128)S(1)} %get-tuple-element.147) | copy-start | bytes 768004
  124.2 6.9 %copy-start.44 = (f32[1,4,125,128]{3,2,1,0:T(8,128)}, f32[1,4,125,128]{3,2,1,0:T(8,128)S(1)}, u32[]{:S(2)}) copy-start(f32[1,4,125,128]{3,2,1,0:T(8,128)S(1)} %get-tuple-element.140) | copy-start | bytes 768004
  124.2 6.9 %copy-start.46 = (f32[1,4,125,128]{3,2,1,0:T(8,128)}, f32[1,4,125,128]{3,2,1,0:T(8,128)S(1)}, u32[]{:S(2)}) copy-start(f32[1,4,125,128]{3,2,1,0:T(8,128)S(1)} %get-tuple-element.143) | copy-start | bytes 768004
  124.3 6.9 %copy-start.48 = (f32[1,4,125,128]{3,2,1,0:T(8,128)}, f32[1,4,125,128]{3,2,1,0:T(8,128)S(1)}, u32[]{:S(2)}) copy-start(f32[1,4,125,128]{3,2,1,0:T(8,128)S(1)} %get-tuple-element.148) | copy-start | bytes 768004
  124.3 6.9 %copy-start.50 = (f32[1,4,125,128]{3,2,1,0:T(8,128)}, f32[1,4,125,128]{3,2,1,0:T(8,128)S(1)}, u32[]{:S(2)}) copy-start(f32[1,4,125,128]{3,2,1,0:T(8,128)S(1)} %get-tuple-element.151) | copy-start | bytes 768004
  124.6 6.6 %copy-start.13 = (f32[1,4,126,128]{3,2,1,0:T(8,128)}, f32[1,4,126,128]{3,2,1,0:T(8,128)S(1)}, u32[]{:S(2)}) copy-start(f32[1,4,126,128]{3,2,1,0:T(8,128)S(1)} %get-tuple-element.159) | copy-start | bytes 774148
  124.6 6.6 %copy-start.14 = (f32[1,4,126,128]{3,2,1,0:T(8,128)}, f32[1,4,126,128]{3,2,1,0:T(8,128)S(1)}, u32[]{:S(2)}) copy-start(f32[1,4,126,128]{3,2,1,0:T(8,128)S(1)} %get-tuple-element.161) | copy-start | bytes 774148
  124.6 6.6 %copy-start.15 = (f32[1,4,126,128]{3,2,1,0:T(8,128)}, f32[1,4,126,128]{3,2,1,0:T(8,128)S(1)}, u32[]{:S(2)}) copy-start(f32[1,4,126,128]{3,2,1,0:T(8,128)S(1)} %get-tuple-element.162) | copy-start | bytes 774148
  124.6 6.6 %copy-start.20 = (f32[1,4,126,128]{3,2,1,0:T(8,128)}, f32[1,4,126,128]{3,2,1,0:T(8,128)S(1)}, u32[]{:S(2)}) copy-start(f32[1,4,126,128]{3,2,1,0:T(8,128)S(1)} %get-tuple-element.160) | copy-start | bytes 774148
  124.6 6.6 %copy-start.22 = (f32[1,4,126,128]{3,2,1,0:T(8,128)}, f32[1,4,126,128]{3,2,1,0:T(8,128)S(1)}, u32[]{:S(2)}) copy-start(f32[1,4,126,128]{3,2,1,0:T(8,128)S(1)} %get-tuple-element.164) | copy-start | bytes 774148
  124.6 6.6 %copy-start.30 = (f32[1,4,126,128]{3,2,1,0:T(8,128)}, f32[1,4,126,128]{3,2,1,0:T(8,128)S(1)}, u32[]{:S(2)}) copy-start(f32[1,4,126,128]{3,2,1,0:T(8,128)S(1)} %get-tuple-element.154) | copy-start | bytes 774148
  124.7 6.6 %copy-start.32 = (f32[1,4,126,128]{3,2,1,0:T(8,128)}, f32[1,4,126,128]{3,2,1,0:T(8,128)S(1)}, u32[]{:S(2)}) copy-start(f32[1,4,126,128]{3,2,1,0:T(8,128)S(1)} %get-tuple-element.157) | copy-start | bytes 774148
  124.7 6.6 %copy-start.34 = (f32[1,4,126,128]{3,2,1,0:T(8,128)}, f32[1,4,126,128]{3,2,1,0:T(8,128)S(1)}, u32[]{:S(2)}) copy-start(f32[1,4,126,128]{3,2,1,0:T(8,128)S(1)} %get-tuple-element.166) | copy-start | bytes 774148
  124.7 6.6 %copy-start.52 = (f32[1,4,126,128]{3,2,1,0:T(8,128)}, f32[1,4,126,128]{3,2,1,0:T(8,128)S(1)}, u32[]{:S(2)}) copy-start(f32[1,4,126,128]{3,2,1,0:T(8,128)S(1)} %get-tuple-element.155) | copy-start | bytes 774148
  125.2 10.2 %copy-start.58 = (f32[1,4,127,128]{3,2,1,0:T(8,128)}, f32[1,4,127,128]{3,2,1,0:T(8,128)S(1)}, u32[]{:S(2)}) copy-start(f32[1,4,127,128]{3,2,1,0:T(8,128)S(1)} %get-tuple-element.172) | copy-start | bytes 780292
  125.2 10.2 %copy-start.60 = (f32[1,4,127,128]{3,2,1,0:T(8,128)}, f32[1,4,127,128]{3,2,1,0:T(8,128)S(1)}, u32[]{:S(2)}) copy-start(f32[1,4,127,128]{3,2,1,0:T(8,128)S(1)} %get-tuple-element.180) | copy-start | bytes 780292
  125.2 10.2 %copy-start.74 = (f32[1,4,3,128]{3,2,1,0:T(4,128)}, f32[1,4,3,128]{3,2,1,0:T(4,128)S(1)}, u32[]{:S(2)}) copy-start(f32[1,4,3,128]{3,2,1,0:T(4,128)S(1)} %get-tuple-element.134) | copy-start | bytes 18436
  125.2 10.2 %copy-start.76 = (f32[1,4,3,128]{3,2,1,0:T(4,128)}, f32[1,4,3,128]{3,2,1,0:T(4,128)S(1)}, u32[]{:S(2)}) copy-start(f32[1,4,3,128]{3,2,1,0:T(4,128)S(1)} %get-tuple-element.135) | copy-start | bytes 18436
  125.2 10.2 %copy-start.78 = (f32[1,4,3,128]{3,2,1,0:T(4,128)}, f32[1,4,3,128]{3,2,1,0:T(4,128)S(1)}, u32[]{:S(2)}) copy-start(f32[1,4,3,128]{3,2,1,0:T(4,128)S(1)} %get-tuple-element.136) | copy-start | bytes 18436
  139.7 34.9 %all-to-all-start = ((bf16[16,1,69,4,128]{4,3,2,1,0:T(4,128)(2,1)}), bf16[16,1,69,4,128]{4,3,2,1,0:T(4,128)(2,1)}, u32[]{:S(2)}, u32[]{:S(2)}) async-start(bf16[16,1,69,4,128]{4,3,2,1,0:T(4,128)(2,1)} %stack.153), calls=%async_computation | async-start | bytes 2260992 | tf_op jit(solution)/shard_map/all_to_all | solution.py:16
  144.5 177.4 %reduce-scatter.5.cloned.1.call-start = ((), (), s32[]{:S(2)}) async-start(), calls=%async_computation.4 | async-start | bytes 270336 | tf_op jit(solution)/shard_map/reduce_scatter | solution.py:222
  204.8 242.1 %reduce-scatter.3.cloned.1.call-start = ((), (), s32[]{:S(2)}) async-start(), calls=%async_computation.3 | async-start | bytes 270336 | tf_op jit(solution)/shard_map/reduce_scatter | solution.py:221
  (78 other events, 194.4 us)
Sparse Core Ops, SparseCore 0:
  204.9 116.9 reduce-scatter.4
  326.5 120.3 reduce-scatter.2
